TPU v7x, 512 devices: a whole 4x4x16 slice. The times are simulated.
512 devices in a mesh: row: 8 (over y, x_hi), col: 16 (over z), layer: 4 (over x_lo, core).
Axes of the slice: x: 4 (x_hi: 2, x_lo: 2; x = x_hi * 2 + x_lo), y: 4, z: 16, core: 2. Of those that a mesh axis runs over, the one named last changes fastest.
Arguments:
- density: bfloat16 [2048, 16384], P('row', ('layer', 'col')), may hold values from -6 to 6
- margin: bfloat16 [16384, 16384], P(('layer', 'row'), 'col'), may hold values from -0.09375 to 0.09375
- block_pattern: int32 [128, 128], replicated, may hold values from 0 to 1, as said below
- atom_functions: int32 [512], replicated, may hold values from 1 to 9, 2048 in all
- atom_kind: int32 [512], P(('row', 'col', 'layer')), may hold values from 0 to 4
- atom_offset: float32 [3, 512], P(None, ('row', 'col', 'layer')), may hold values from 0 to 128, as said below
- exponents: float32 [5], replicated, may hold values from 0.02 to 1
Outputs:
- density_product: bfloat16 [2048, 16384], P('row', ('col', 'layer'))
- electron_density: float32 [256, 512, 512], P('row', 'col', 'layer')
Inputs may be any that keep to these rules, and one draw needn't show every extreme that they name: `block_pattern`: symmetric, with ones on its diagonal; block_pattern[i, j] = 0 whenever |i - j| > 32 (no block couples to one more than 32 blocks away). `atom_functions`: all atoms' functions together are the 2048 rows of the window. `atom_offset`: row k of an atom lies in [0, the tile's cells along dimension k), that is 32, 32 or 128.
All inputs are finite; a program needn't handle non-finite values.
Results may differ from a plain program's by a relative error of at most 0.001.
Values may be sent and summed in bfloat16 or wider, within the bound.
A program may use at most 64 MiB of HBM per device.

v0:
```python
import jax
import jax.numpy as jnp
from jax import lax
from jax.sharding import PartitionSpec as P

BLK = 128
TX = 32
TY = 32
TZ = 128
HALO = 16


def passed_along(block, axis, distance):
    devices = range(lax.axis_size(axis))
    route = [((i - distance) % len(devices), i) for i in devices]
    return lax.ppermute(block, axis, route)


def with_halo(block, sides, width):
    for axis, dim in sides:
        count = lax.axis_size(axis)
        forward = [(i, i + 1) for i in range(count - 1)]
        forward.append((count - 1, 0))
        backward = [(target, source) for source, target in forward]
        low = lax.ppermute(
            lax.slice_in_dim(block, block.shape[dim] - width, None, axis=dim), axis, forward
        )
        high = lax.ppermute(lax.slice_in_dim(block, 0, width, axis=dim), axis, backward)
        block = jnp.concatenate([low, block, high], axis=dim)
    return block


def apply_pattern(matrix, pattern_part):
    row_blocks = matrix.shape[0] // BLK
    col_blocks = matrix.shape[1] // BLK
    shaped = matrix.reshape(row_blocks, BLK, col_blocks, BLK)
    gate_mask = pattern_part.astype(jnp.bfloat16)
    return (shaped * gate_mask[:, None, :, None]).reshape(matrix.shape)


def local_profile(offset, exponent_of, extent):
    local_cells = jnp.arange(-HALO, extent + HALO, dtype=jnp.int32).astype(jnp.float32)
    distance = local_cells[None, :] - offset[:, None]
    return jnp.where(
        jnp.abs(distance) <= HALO, jnp.exp(-exponent_of[:, None] * distance * distance), 0.0
    )


def fold_rims(values_in, axis_dim, extent):
    middle = lax.slice_in_dim(values_in, 2 * HALO, 2 * HALO + extent, axis=axis_dim)
    lower_rim = lax.slice_in_dim(values_in, 0, HALO, axis=axis_dim)
    upper_rim = lax.slice_in_dim(values_in, extent + 3 * HALO, extent + 4 * HALO, axis=axis_dim)
    lower_edge = lax.slice_in_dim(middle, 0, HALO, axis=axis_dim) + lower_rim
    upper_edge = lax.slice_in_dim(middle, extent - HALO, extent, axis=axis_dim) + upper_rim
    inner_part = lax.slice_in_dim(middle, HALO, extent - HALO, axis=axis_dim)
    return jnp.concatenate([lower_edge, inner_part, upper_edge], axis=axis_dim)


def kind_exponent(kinds_of, exponents):
    kind_match = kinds_of[:, None] == jnp.arange(exponents.shape[0], dtype=jnp.int32)[None, :]
    return jnp.sum(jnp.where(kind_match, exponents[None, :], 0.0), axis=1)


def shards(density, margin, block_pattern, atom_functions, atom_kind, atom_offset, exponents):
    rows_here, piece_width = density.shape
    share_rows, share_cols = margin.shape
    n_row = lax.axis_size("row")
    n_col = lax.axis_size("col")
    n_layer = lax.axis_size("layer")
    row_index = lax.axis_index("row")
    col_index = lax.axis_index("col")
    layer_index = lax.axis_index("layer")
    density_mask = lax.dynamic_slice(
        block_pattern,
        (row_index * (rows_here // BLK), (layer_index * n_col + col_index) * piece_width // BLK),
        (rows_here // BLK, piece_width // BLK),
    )
    masked = apply_pattern(density, density_mask)
    margin_mask = lax.dynamic_slice(
        block_pattern,
        ((layer_index * n_row + row_index) * share_rows // BLK, col_index * share_cols // BLK),
        (share_rows // BLK, share_cols // BLK),
    )
    margin_masked = apply_pattern(margin, margin_mask)
    columns_panel = lax.all_gather(margin_masked, "row", axis=0, tiled=True)

    def add_piece(running, piece_rows, first_row):
        rows_of = lax.dynamic_slice_in_dim(columns_panel, first_row, piece_rows.shape[1], 0)
        return running + jnp.dot(piece_rows, rows_of, preferred_element_type=jnp.float32)

    product_zero = jnp.zeros((rows_here, share_cols), jnp.float32)

    def advance_one(turn_index, state_tuple):
        moving, running = state_tuple
        moving = passed_along(moving, "col", 1)
        return (
            moving,
            add_piece(running, moving, (col_index - turn_index - 1) % n_col * piece_width),
        )

    start_sum = add_piece(product_zero, masked, col_index * piece_width)
    product_acc = lax.fori_loop(0, n_col - 1, advance_one, (masked, start_sum))[1]
    product = lax.psum_scatter(product_acc, "layer", scatter_dimension=1, tiled=True)
    strip_width = product.shape[1]
    rows_global = row_index * rows_here + jnp.arange(rows_here, dtype=jnp.int32)
    cols_global = (col_index * n_layer + layer_index) * strip_width + jnp.arange(
        strip_width, dtype=jnp.int32
    )
    on_diagonal = rows_global[:, None] == cols_global[None, :]
    diagonal_part = jnp.sum(jnp.where(on_diagonal, product, 0.0), axis=0)
    run_ends = jnp.cumsum(atom_functions, dtype=jnp.int32)
    run_starts = run_ends - atom_functions
    member = (cols_global[:, None] >= run_starts[None, :]) & (
        cols_global[:, None] < run_ends[None, :]
    )
    partial_pop = jnp.dot(
        diagonal_part, member.astype(jnp.float32), precision=lax.Precision.HIGHEST
    )
    all_pop = lax.psum(partial_pop, ("row", "col", "layer"))
    slot_count = atom_kind.shape[0]
    tile_index = (row_index * n_col + col_index) * n_layer + layer_index
    own_pop = lax.dynamic_slice_in_dim(all_pop, tile_index * slot_count, slot_count, 0)
    exponent_of = kind_exponent(atom_kind, exponents)
    weight_x = own_pop[:, None] * local_profile(atom_offset[0], exponent_of, TX)
    along_y = local_profile(atom_offset[1], exponent_of, TY)
    along_z = local_profile(atom_offset[2], exponent_of, TZ)
    paired = weight_x[:, :, None] * along_y[:, None, :]
    extended = jnp.einsum("axy,az->xyz", paired, along_z, precision=lax.Precision.HIGHEST)
    summed = with_halo(extended, (("row", 0), ("col", 1), ("layer", 2)), HALO)
    electron_density = fold_rims(fold_rims(fold_rims(summed, 0, TX), 1, TY), 2, TZ)
    return (product.astype(jnp.bfloat16), electron_density)


def solution(mesh):
    placed = (
        P("row", ("layer", "col")),
        P(("layer", "row"), "col"),
        P(),
        P(),
        P(("row", "col", "layer")),
        P(None, ("row", "col", "layer")),
        P(),
    )
    return jax.shard_map(
        shards,
        mesh=mesh,
        in_specs=placed,
        out_specs=(P("row", ("col", "layer")), P("row", "col", "layer")),
        check_vma=False,
    )
```

profile of v0, /device:TPU:1, one launch (start us, length us, event | category | flops | bytes accessed | tf_op | source)
XLA Modules:
  0.0 577.8 jit_solution(15590409641228112352)
XLA Ops:
  10.6 127.0 %all-gather.2.cloned.1.call-done = bf16[4096,1024]{1,0:T(8,128)(2,1)} async-done(((bf16[512,1024]{1,0:T(8,128)(2,1)}), bf16[4096,1024]{1,0:T(8,128)(2,1)}) %all-gather.2.cloned.1.call-update) | async-done | bytes 8388624 | tf_op jit(solution)/shard_map/all_gather | solution.py:85
  139.1 129.6 %while.17 = (s32[]{:T(128)}, bf16[256,256]{1,0:T(8,128)(2,1)S(1)}, f32[256,1024]{0,1:T(8,128)S(1)}, s32[]{:T(128)}, bf16[4096,1024]{1,0:T(8,128)(2,1)}, /*index=...) while((s32[]{:T(128)}, bf16[256,256]{1,0:T(8,128)(2,1)S(1)}, ...), condition=%wide.region_1.2_spmd, body=%wide.region_0.1_spmd.sunk | while | flops 134479888 | bytes 3539284 | solution.py:102
  139.1 3.2 collective-permute-start
  142.3 4.8 collective-permute-done
  148.6 1.9 collective-permute-start
  150.5 5.0 collective-permute-done
  157.0 1.9 collective-permute-start
  158.9 5.0 collective-permute-done
  165.3 1.9 collective-permute-start
  167.3 5.0 collective-permute-done
  175.7 5.0 collective-permute-done
  184.1 5.0 collective-permute-done
  192.4 5.3 collective-permute-done
  201.2 6.6 %collective-permute-done = bf16[256,256]{1,0:T(8,128)(2,1)S(1)} collective-permute-done((bf16[256,256]{1,0:T(8,128)(2,1)S(1)}, bf16[256,256]{1,0:T(8,128)(2,1)S(1)}, u32[]{:S(2)}, u32[]{:S(2)}) %collective-permute-start) | collective-permute-done | bytes 131104 | tf_op jit(solution)/shard_map/while/body/eval_jaxpr/ppermute | solution.py:16
  211.2 5.7 collective-permute-done
  220.3 5.0 collective-permute-done
  228.7 5.0 collective-permute-done
  235.1 1.9 collective-permute-start
  237.1 5.0 collective-permute-done
  245.5 5.0 collective-permute-done
  253.8 5.0 collective-permute-done
  262.2 5.0 collective-permute-done
  274.5 38.1 %reduce-scatter.2.cloned.1.call-done = f32[256,256]{1,0:T(8,128)} async-done(((f32[256,1024]{1,0:T(8,128)}), f32[256,256]{1,0:T(8,128)}) %reduce-scatter.2.cloned.1.call-update) | async-done | bytes 262160 | tf_op jit(solution)/shard_map/reduce_scatter | solution.py:103
  314.7 105.2 %psum.7 = f32[512]{0:T(512)S(1)} all-reduce(f32[512]{0:T(512)S(1)} %bitcast.36), channel_id=1, replica_groups=mesh['row'=8,'col'=16,'layer'=4] {'row','col','layer'}, use_global_device_ids=true, to_apply=%region_6.7 | all-reduce | flops 512 | bytes 4096 | tf_op jit(solution)/shard_map/psum | solution.py:119
  422.5 3.1 collective-permute-start.1
  425.6 5.8 %collective-permute-start.2 = (f32[16,64,160]{2,1,0:T(8,128)S(1)}, f32[16,64,160]{2,1,0:T(8,128)S(1)}, u32[]{:S(2)}, u32[]{:S(2)}) collective-permute-start(f32[16,64,160]{2,1,0:T(8,128)S(1)} %get-tuple-element.176), channel_id=1, source_target_pairs={{64,0},{128,64},{192,128},{256,192},{320,256},{384,320},{448,384},... | collective-permute-start | bytes 1966088 | tf_op jit(solution)/shard_map/ppermute | solution.py:28
  431.4 20.6 %collective-permute-done.1 = f32[16,64,160]{2,1,0:T(8,128)S(1)} collective-permute-done((f32[16,64,160]{2,1,0:T(8,128)S(1)}, f32[16,64,160]{2,1,0:T(8,128)S(1)}, u32[]{:S(2)}, u32[]{:S(2)}) %collective-permute-start.1) | collective-permute-done | bytes 655392 | tf_op jit(solution)/shard_map/ppermute | solution.py:25
  452.1 19.8 %collective-permute-done.2 = f32[16,64,160]{2,1,0:T(8,128)S(1)} collective-permute-done((f32[16,64,160]{2,1,0:T(8,128)S(1)}, f32[16,64,160]{2,1,0:T(8,128)S(1)}, u32[]{:S(2)}, u32[]{:S(2)}) %collective-permute-start.2) | collective-permute-done | bytes 655392 | tf_op jit(solution)/shard_map/ppermute | solution.py:28
  473.4 3.3 copy.23
  476.7 2.9 collective-permute-start.4
  479.7 2.1 copy.22
  481.8 2.4 collective-permute-start.3
  484.1 23.6 %collective-permute-done.4 = f32[96,16,160]{0,2,1:T(8,128)} collective-permute-done((f32[96,16,160]{0,2,1:T(8,128)}, f32[96,16,160]{0,2,1:T(8,128)}, u32[]{:S(2)}, u32[]{:S(2)}) %collective-permute-start.4) | collective-permute-done | bytes 983072 | tf_op jit(solution)/shard_map/ppermute | solution.py:28
  507.7 2.6 copy.25
  510.3 3.4 collective-permute-done.3
  513.7 3.6 copy.24
  517.3 3.7 pad_maximum_fusion
  521.0 5.3 fusion.24
  526.3 3.8 copy.26
  530.1 4.2 collective-permute-start.5
  534.3 3.8 copy.27
  538.1 2.5 collective-permute-start.6
  540.6 3.3 collective-permute-done.5
  543.9 3.8 copy.28
  547.7 6.4 %collective-permute-done.6 = f32[96,96,16]{1,2,0:T(8,128)} collective-permute-done((f32[96,96,16]{1,2,0:T(8,128)}, f32[96,96,16]{1,2,0:T(8,128)}, u32[]{:S(2)}, u32[]{:S(2)}) %collective-permute-start.6) | collective-permute-done | bytes 589856 | tf_op jit(solution)/shard_map/ppermute | solution.py:28
  554.1 3.9 copy.29
  558.0 5.8 %maximum_add_fusion = f32[16,96,192]{2,1,0:T(8,128)S(1)} fusion(f32[96,96,16]{2,1,0:T(8,128)} %copy.29, f32[96,96,16]{2,1,0:T(8,128)} %copy.28, f32[96,16,160]{2,1,0:T(8,128)S(1)} %copy.25, f32[96,16,160]{2,1,0:T(8,128)} %copy.24, f32[16,64,160]{2,1,0:T(8,128)} %copy-done.4, f32[64,64,160]{2,1,0:T(8,128)} %copy-done, ...), kind=kLoop, calls=%fused_computation.21 | loop fusion | flops 3833856 | bytes 8257536 | tf_op jit(solution)/shard_map/add | solution.py:53
  564.9 4.0 fusion.3
  (101 shorter events, 59.3 us)
Async XLA Ops:
  7.2 1.2 copy-start.6
  7.2 130.5 %all-gather.2.cloned.1.call-start = ((), (), s32[]{:S(2)}) async-start(), calls=%async_computation.1 | async-start | bytes 9437184 | tf_op jit(solution)/shard_map/all_gather | solution.py:85
  8.4 2.2 copy-start.7
  9.6 303.0 %reduce-scatter.2.cloned.1.call-start = ((), (), s32[]{:S(2)}) async-start(), calls=%async_computation.2 | async-start | bytes 1310720 | tf_op jit(solution)/shard_map/reduce_scatter | solution.py:103
  139.1 8.0 %collective-permute-start = (bf16[256,256]{1,0:T(8,128)(2,1)S(1)}, bf16[256,256]{1,0:T(8,128)(2,1)S(1)}, u32[]{:S(2)}, u32[]{:S(2)}) collective-permute-start(bf16[256,256]{1,0:T(8,128)(2,1)S(1)} %get-tuple-element.232), channel_id=1, source_target_pairs={{60,0},{0,4},{4,8},{8,12},{12,16},{16,20},{20,24},{24,28},{28,32},... | collective-permute-start | bytes 393224 | tf_op jit(solution)/shard_map/while/body/eval_jaxpr/ppermute | solution.py:16
  148.6 6.9 %collective-permute-start = (bf16[256,256]{1,0:T(8,128)(2,1)S(1)}, bf16[256,256]{1,0:T(8,128)(2,1)S(1)}, u32[]{:S(2)}, u32[]{:S(2)}) collective-permute-start(bf16[256,256]{1,0:T(8,128)(2,1)S(1)} %get-tuple-element.232), channel_id=1, source_target_pairs={{60,0},{0,4},{4,8},{8,12},{12,16},{16,20},{20,24},{24,28},{28,32},... | collective-permute-start | bytes 393224 | tf_op jit(solution)/shard_map/while/body/eval_jaxpr/ppermute | solution.py:16
  157.0 6.9 %collective-permute-start = (bf16[256,256]{1,0:T(8,128)(2,1)S(1)}, bf16[256,256]{1,0:T(8,128)(2,1)S(1)}, u32[]{:S(2)}, u32[]{:S(2)}) collective-permute-start(bf16[256,256]{1,0:T(8,128)(2,1)S(1)} %get-tuple-element.232), channel_id=1, source_target_pairs={{60,0},{0,4},{4,8},{8,12},{12,16},{16,20},{20,24},{24,28},{28,32},... | collective-permute-start | bytes 393224 | tf_op jit(solution)/shard_map/while/body/eval_jaxpr/ppermute | solution.py:16
  165.3 6.9 %collective-permute-start = (bf16[256,256]{1,0:T(8,128)(2,1)S(1)}, bf16[256,256]{1,0:T(8,128)(2,1)S(1)}, u32[]{:S(2)}, u32[]{:S(2)}) collective-permute-start(bf16[256,256]{1,0:T(8,128)(2,1)S(1)} %get-tuple-element.232), channel_id=1, source_target_pairs={{60,0},{0,4},{4,8},{8,12},{12,16},{16,20},{20,24},{24,28},{28,32},... | collective-permute-start | bytes 393224 | tf_op jit(solution)/shard_map/while/body/eval_jaxpr/ppermute | solution.py:16
  173.7 6.9 %collective-permute-start = (bf16[256,256]{1,0:T(8,128)(2,1)S(1)}, bf16[256,256]{1,0:T(8,128)(2,1)S(1)}, u32[]{:S(2)}, u32[]{:S(2)}) collective-permute-start(bf16[256,256]{1,0:T(8,128)(2,1)S(1)} %get-tuple-element.232), channel_id=1, source_target_pairs={{60,0},{0,4},{4,8},{8,12},{12,16},{16,20},{20,24},{24,28},{28,32},... | collective-permute-start | bytes 393224 | tf_op jit(solution)/shard_map/while/body/eval_jaxpr/ppermute | solution.py:16
  182.1 6.9 %collective-permute-start = (bf16[256,256]{1,0:T(8,128)(2,1)S(1)}, bf16[256,256]{1,0:T(8,128)(2,1)S(1)}, u32[]{:S(2)}, u32[]{:S(2)}) collective-permute-start(bf16[256,256]{1,0:T(8,128)(2,1)S(1)} %get-tuple-element.232), channel_id=1, source_target_pairs={{60,0},{0,4},{4,8},{8,12},{12,16},{16,20},{20,24},{24,28},{28,32},... | collective-permute-start | bytes 393224 | tf_op jit(solution)/shard_map/while/body/eval_jaxpr/ppermute | solution.py:16
  190.5 7.3 %collective-permute-start = (bf16[256,256]{1,0:T(8,128)(2,1)S(1)}, bf16[256,256]{1,0:T(8,128)(2,1)S(1)}, u32[]{:S(2)}, u32[]{:S(2)}) collective-permute-start(bf16[256,256]{1,0:T(8,128)(2,1)S(1)} %get-tuple-element.232), channel_id=1, source_target_pairs={{60,0},{0,4},{4,8},{8,12},{12,16},{16,20},{20,24},{24,28},{28,32},... | collective-permute-start | bytes 393224 | tf_op jit(solution)/shard_map/while/body/eval_jaxpr/ppermute | solution.py:16
  199.2 8.5 %collective-permute-start = (bf16[256,256]{1,0:T(8,128)(2,1)S(1)}, bf16[256,256]{1,0:T(8,128)(2,1)S(1)}, u32[]{:S(2)}, u32[]{:S(2)}) collective-permute-start(bf16[256,256]{1,0:T(8,128)(2,1)S(1)} %get-tuple-element.232), channel_id=1, source_target_pairs={{60,0},{0,4},{4,8},{8,12},{12,16},{16,20},{20,24},{24,28},{28,32},... | collective-permute-start | bytes 393224 | tf_op jit(solution)/shard_map/while/body/eval_jaxpr/ppermute | solution.py:16
  209.2 7.7 %collective-permute-start = (bf16[256,256]{1,0:T(8,128)(2,1)S(1)}, bf16[256,256]{1,0:T(8,128)(2,1)S(1)}, u32[]{:S(2)}, u32[]{:S(2)}) collective-permute-start(bf16[256,256]{1,0:T(8,128)(2,1)S(1)} %get-tuple-element.232), channel_id=1, source_target_pairs={{60,0},{0,4},{4,8},{8,12},{12,16},{16,20},{20,24},{24,28},{28,32},... | collective-permute-start | bytes 393224 | tf_op jit(solution)/shard_map/while/body/eval_jaxpr/ppermute | solution.py:16
  218.3 6.9 %collective-permute-start = (bf16[256,256]{1,0:T(8,128)(2,1)S(1)}, bf16[256,256]{1,0:T(8,128)(2,1)S(1)}, u32[]{:S(2)}, u32[]{:S(2)}) collective-permute-start(bf16[256,256]{1,0:T(8,128)(2,1)S(1)} %get-tuple-element.232), channel_id=1, source_target_pairs={{60,0},{0,4},{4,8},{8,12},{12,16},{16,20},{20,24},{24,28},{28,32},... | collective-permute-start | bytes 393224 | tf_op jit(solution)/shard_map/while/body/eval_jaxpr/ppermute | solution.py:16
  226.7 6.9 %collective-permute-start = (bf16[256,256]{1,0:T(8,128)(2,1)S(1)}, bf16[256,256]{1,0:T(8,128)(2,1)S(1)}, u32[]{:S(2)}, u32[]{:S(2)}) collective-permute-start(bf16[256,256]{1,0:T(8,128)(2,1)S(1)} %get-tuple-element.232), channel_id=1, source_target_pairs={{60,0},{0,4},{4,8},{8,12},{12,16},{16,20},{20,24},{24,28},{28,32},... | collective-permute-start | bytes 393224 | tf_op jit(solution)/shard_map/while/body/eval_jaxpr/ppermute | solution.py:16
  235.1 6.9 %collective-permute-start = (bf16[256,256]{1,0:T(8,128)(2,1)S(1)}, bf16[256,256]{1,0:T(8,128)(2,1)S(1)}, u32[]{:S(2)}, u32[]{:S(2)}) collective-permute-start(bf16[256,256]{1,0:T(8,128)(2,1)S(1)} %get-tuple-element.232), channel_id=1, source_target_pairs={{60,0},{0,4},{4,8},{8,12},{12,16},{16,20},{20,24},{24,28},{28,32},... | collective-permute-start | bytes 393224 | tf_op jit(solution)/shard_map/while/body/eval_jaxpr/ppermute | solution.py:16
  243.5 6.9 %collective-permute-start = (bf16[256,256]{1,0:T(8,128)(2,1)S(1)}, bf16[256,256]{1,0:T(8,128)(2,1)S(1)}, u32[]{:S(2)}, u32[]{:S(2)}) collective-permute-start(bf16[256,256]{1,0:T(8,128)(2,1)S(1)} %get-tuple-element.232), channel_id=1, source_target_pairs={{60,0},{0,4},{4,8},{8,12},{12,16},{16,20},{20,24},{24,28},{28,32},... | collective-permute-start | bytes 393224 | tf_op jit(solution)/shard_map/while/body/eval_jaxpr/ppermute | solution.py:16
  251.9 6.9 %collective-permute-start = (bf16[256,256]{1,0:T(8,128)(2,1)S(1)}, bf16[256,256]{1,0:T(8,128)(2,1)S(1)}, u32[]{:S(2)}, u32[]{:S(2)}) collective-permute-start(bf16[256,256]{1,0:T(8,128)(2,1)S(1)} %get-tuple-element.232), channel_id=1, source_target_pairs={{60,0},{0,4},{4,8},{8,12},{12,16},{16,20},{20,24},{24,28},{28,32},... | collective-permute-start | bytes 393224 | tf_op jit(solution)/shard_map/while/body/eval_jaxpr/ppermute | solution.py:16
  260.3 6.9 %collective-permute-start = (bf16[256,256]{1,0:T(8,128)(2,1)S(1)}, bf16[256,256]{1,0:T(8,128)(2,1)S(1)}, u32[]{:S(2)}, u32[]{:S(2)}) collective-permute-start(bf16[256,256]{1,0:T(8,128)(2,1)S(1)} %get-tuple-element.232), channel_id=1, source_target_pairs={{60,0},{0,4},{4,8},{8,12},{12,16},{16,20},{20,24},{24,28},{28,32},... | collective-permute-start | bytes 393224 | tf_op jit(solution)/shard_map/while/body/eval_jaxpr/ppermute | solution.py:16
  268.6 2.0 copy-start.10
  268.7 3.3 copy-start.8
  268.7 3.7 copy-start.9
  422.4 49.5 %copy-start = (f32[64,64,160]{2,1,0:T(8,128)}, f32[64,64,160]{2,1,0:T(8,128)S(1)}, u32[]{:S(2)}) copy-start(f32[64,64,160]{2,1,0:T(8,128)S(1)} %broadcast_multiply_fusion) | copy-start | bytes 7864324
  422.5 29.6 %collective-permute-start.1 = (f32[16,64,160]{2,1,0:T(8,128)S(1)}, f32[16,64,160]{2,1,0:T(8,128)S(1)}, u32[]{:S(2)}, u32[]{:S(2)}) collective-permute-start(f32[16,64,160]{2,1,0:T(8,128)S(1)} %get-tuple-element.175), channel_id=1, source_target_pairs={{0,64},{64,128},{128,192},{192,256},{256,320},{320,384},{384,448},... | collective-permute-start | bytes 1966088 | tf_op jit(solution)/shard_map/ppermute | solution.py:25
  425.6 46.3 %collective-permute-start.2 = (f32[16,64,160]{2,1,0:T(8,128)S(1)}, f32[16,64,160]{2,1,0:T(8,128)S(1)}, u32[]{:S(2)}, u32[]{:S(2)}) collective-permute-start(f32[16,64,160]{2,1,0:T(8,128)S(1)} %get-tuple-element.176), channel_id=1, source_target_pairs={{64,0},{128,64},{192,128},{256,192},{320,256},{384,320},{448,384},... | collective-permute-start | bytes 1966088 | tf_op jit(solution)/shard_map/ppermute | solution.py:28
  471.9 1.6 copy-start.4
  476.7 31.0 %collective-permute-start.4 = (f32[96,16,160]{0,2,1:T(8,128)}, f32[96,16,160]{0,2,1:T(8,128)}, u32[]{:S(2)}, u32[]{:S(2)}) collective-permute-start(f32[96,16,160]{0,2,1:T(8,128)} %copy.23), channel_id=1, source_target_pairs={{4,0},{8,4},{12,8},{16,12},{20,16},{24,20},{28,24},{32,28},{36,32}... | collective-permute-start | bytes 2949128 | tf_op jit(solution)/shard_map/ppermute | solution.py:28
  481.8 31.9 %collective-permute-start.3 = (f32[96,16,160]{0,2,1:T(8,128)}, f32[96,16,160]{0,2,1:T(8,128)}, u32[]{:S(2)}, u32[]{:S(2)}) collective-permute-start(f32[96,16,160]{0,2,1:T(8,128)} %copy.22), channel_id=1, source_target_pairs={{0,4},{4,8},{8,12},{12,16},{16,20},{20,24},{24,28},{28,32},{32,36}... | collective-permute-start | bytes 2949128 | tf_op jit(solution)/shard_map/ppermute | solution.py:25
  530.1 13.8 %collective-permute-start.5 = (f32[96,96,16]{1,2,0:T(8,128)}, f32[96,96,16]{1,2,0:T(8,128)}, u32[]{:S(2)}, u32[]{:S(2)}) collective-permute-start(f32[96,96,16]{1,2,0:T(8,128)} %copy.26), channel_id=1, source_target_pairs={{0,1},{1,2},{2,3},{3,0},{4,5},{5,6},{6,7},{7,4},{8,9},{9,10},{10,1... | collective-permute-start | bytes 1769480 | tf_op jit(solution)/shard_map/ppermute | solution.py:25
  538.1 16.0 %collective-permute-start.6 = (f32[96,96,16]{1,2,0:T(8,128)}, f32[96,96,16]{1,2,0:T(8,128)}, u32[]{:S(2)}, u32[]{:S(2)}) collective-permute-start(f32[96,96,16]{1,2,0:T(8,128)} %copy.27), channel_id=1, source_target_pairs={{1,0},{2,1},{3,2},{0,3},{5,4},{6,5},{7,6},{4,7},{9,8},{10,9},{11,1... | collective-permute-start | bytes 1769480 | tf_op jit(solution)/shard_map/ppermute | solution.py:28
  554.1 9.8 %slice-start = ((s8[4718592]{0:T(1024)(128)(4,1)}), s8[524288]{0:T(1024)(128)(4,1)S(1)}, s32[]{:S(2)}) async-start(s8[4718592]{0:T(1024)(128)(4,1)} %bitcast.31), calls=%async_computation.3 | async-start | bytes 1048576
  558.0 5.9 %copy-start.1 = (f32[64,64,160]{2,1,0:T(8,128)S(1)}, f32[64,64,160]{2,1,0:T(8,128)}, u32[]{:S(2)}) copy-start(f32[64,64,160]{2,1,0:T(8,128)} %copy-done) | copy-start | bytes 7864324
  558.0 5.9 %slice-start.1 = ((s8[4718592]{0:T(1024)(128)(4,1)}), s8[4194304]{0:T(1024)(128)(4,1)S(1)}, s32[]{:S(2)}) async-start(s8[4718592]{0:T(1024)(128)(4,1)} %bitcast.31), calls=%async_computation.4 | async-start | bytes 8388608
  558.0 6.2 %copy-start.2 = (f32[96,96,16]{2,1,0:T(8,128)S(1)}, f32[96,96,16]{2,1,0:T(8,128)}, u32[]{:S(2)}) copy-start(f32[96,96,16]{2,1,0:T(8,128)} %copy.29) | copy-start | bytes 1769476
  558.0 6.6 %copy-start.3 = (f32[96,16,160]{2,1,0:T(8,128)S(1)}, f32[96,16,160]{2,1,0:T(8,128)}, u32[]{:S(2)}) copy-start(f32[96,16,160]{2,1,0:T(8,128)} %copy.24) | copy-start | bytes 2949124
  558.0 6.9 %copy-start.5 = (f32[16,64,160]{2,1,0:T(8,128)S(1)}, f32[16,64,160]{2,1,0:T(8,128)}, u32[]{:S(2)}) copy-start(f32[16,64,160]{2,1,0:T(8,128)} %copy-done.4) | copy-start | bytes 1966084
Sparse Core Ops, SparseCore 0:
  11.2 126.4 all-gather.1
  270.1 42.3 reduce-scatter.1
where the time goes:
time: 580 us; the launch traced here: 578 us
  waiting for transfers between devices  319 us (55%)
  blocking collectives  105 us (18%)
  starting transfers between devices  51 us (9%)
  local copies, waits for them, and re-layouts  36.6 us (6%)
  other arithmetic  25.9 us (4%)
  matrix products  23.1 us (4%)
  between operations  15.7 us (3%)
    all_gather x1, waiting for transfers between devices, shards(): columns_panel = lax.all_gather(margin_masked, 'row', axis=0, tiled=True)  127 us
    psum x1, blocking collectives, shards(): all_pop = lax.psum(partial_pop, ('row', 'col', 'layer'))  105 us
    ppermute x15, waiting for transfers between devices, passed_along(): return lax.ppermute(block, axis, route)  77.1 us
    ppermute x3, waiting for transfers between devices, with_halo(): lax.ppermute(lax.slice_in_dim(block, 0, width, axis=dim), axis, backward)  49.8 us
    reduce_scatter x1, waiting for transfers between devices, shards(): lax.psum_scatter(product_acc, 'layer', scatter_dimension=1, tiled=True)  38.1 us
    ppermute x15, starting transfers between devices, passed_along(): return lax.ppermute(block, axis, route)  30.1 us
    ppermute x3, waiting for transfers between devices, with_halo(): lax.ppermute(lax.slice_in_dim(block, block.shape[dim] - width, None, axis...  27.3 us
    dot_general x16, matrix products, add_piece(): jnp.dot(piece_rows, rows_of, preferred_element_type=jnp.float32)  22.8 us
  transfers between devices with their start and end apart: 23, of which 23 were waited for; matrix products, arithmetic and copies ran while one was open for 3% of the time, Pallas kernels for 0%

commit v1 on v0

--- a/solution.py
+++ b/solution.py
@@ -82,7 +82,9 @@
         (share_rows // BLK, share_cols // BLK),
     )
     margin_masked = apply_pattern(margin, margin_mask)
-    columns_panel = lax.all_gather(margin_masked, "row", axis=0, tiled=True)
+    columns_panel = jnp.concatenate(
+        lax.all_to_all(jnp.stack([margin_masked] * lax.axis_size("row")), "row", 0, 0), axis=0
+    )
 
     def add_piece(running, piece_rows, first_row):
         rows_of = lax.dynamic_slice_in_dim(columns_panel, first_row, piece_rows.shape[1], 0)

time: 580 us -> 561 us (0.967)
  waiting for transfers between devices: 319 us -> 286 us
  starting transfers between devices: 51 us -> 62.2 us
    all_gather x1 -> x0, waiting for transfers between devices: 127 us -> none  [shards(): columns_panel = lax.all_gather(margin_masked, 'row', axis=0, tiled=True)]
    all_to_all x0 -> x1, waiting for transfers between devices: none -> 90.8 us  [shards(): lax.all_to_all(jnp.stack([margin_masked] * lax.axis_size('row')), 'row',...]
    all_to_all x0 -> x1, starting transfers between devices: none -> 7.6 us  [shards(): lax.all_to_all(jnp.stack([margin_masked] * lax.axis_size('row')), 'row',...]
where the time goes in v1:
time: 561 us; the launch traced here: 559 us
  waiting for transfers between devices  286 us (51%)
  blocking collectives  105 us (19%)
  starting transfers between devices  62.2 us (11%)
  local copies, waits for them, and re-layouts  41.1 us (7%)
  other arithmetic  24.9 us (4%)
  matrix products  23.1 us (4%)
  between operations  15.7 us (3%)
    psum x1, blocking collectives, shards(): all_pop = lax.psum(partial_pop, ('row', 'col', 'layer'))  105 us
    all_to_all x1, waiting for transfers between devices, shards(): lax.all_to_all(jnp.stack([margin_masked] * lax.axis_size('row')), 'row',...  90.8 us
    ppermute x15, waiting for transfers between devices, passed_along(): return lax.ppermute(block, axis, route)  81.7 us
    ppermute x3, waiting for transfers between devices, with_halo(): lax.ppermute(lax.slice_in_dim(block, 0, width, axis=dim), axis, backward)  50 us
    reduce_scatter x1, waiting for transfers between devices, shards(): lax.psum_scatter(product_acc, 'layer', scatter_dimension=1, tiled=True)  36.2 us
    ppermute x15, starting transfers between devices, passed_along(): return lax.ppermute(block, axis, route)  33.7 us
    ppermute x3, waiting for transfers between devices, with_halo(): lax.ppermute(lax.slice_in_dim(block, block.shape[dim] - width, None, axis...  27.2 us
    dot_general x16, matrix products, add_piece(): jnp.dot(piece_rows, rows_of, preferred_element_type=jnp.float32)  22.8 us
  transfers between devices with their start and end apart: 23, of which 23 were waited for; matrix products, arithmetic and copies ran while one was open for 3% of the time, Pallas kernels for 0%

profile of v1, /device:TPU:1, one launch (start us, length us, event | category | flops | bytes accessed | tf_op | source)
XLA Modules:
  0.0 559.0 jit_solution(1104193049051275824)
XLA Ops:
  8.5 4.3 stack.3
  12.9 7.6 %all-to-all-start = ((bf16[8,512,1024]{2,1,0:T(8,128)(2,1)}), bf16[8,512,1024]{2,1,0:T(8,128)(2,1)}, u32[]{:S(2)}, u32[]{:S(2)}) async-start(bf16[8,512,1024]{2,1,0:T(8,128)(2,1)} %stack.3), calls=%async_computation | async-start | bytes 16777216 | tf_op jit(solution)/shard_map/all_to_all | solution.py:86
  21.5 90.8 %all-to-all-done = bf16[8,512,1024]{2,1,0:T(8,128)(2,1)} async-done(((bf16[8,512,1024]{2,1,0:T(8,128)(2,1)}), bf16[8,512,1024]{2,1,0:T(8,128)(2,1)}, u32[]{:S(2)}, u32[]{:S(2)}) %all-to-all-start) | async-done | bytes 8388640 | tf_op jit(solution)/shard_map/all_to_all | solution.py:86
  113.7 137.8 %while.17 = (s32[]{:T(128)}, bf16[256,256]{1,0:T(8,128)(2,1)S(1)}, f32[256,1024]{0,1:T(8,128)S(1)}, s32[]{:T(128)}, bf16[4096,1024]{1,0:T(8,128)(2,1)}, /*index=...) while((s32[]{:T(128)}, bf16[256,256]{1,0:T(8,128)(2,1)S(1)}, ...), condition=%wide.region_1.2_spmd, body=%wide.region_0.1_spmd.sunk | while | flops 134479888 | bytes 3539284 | solution.py:104
  113.7 6.8 %collective-permute-start = (bf16[256,256]{1,0:T(8,128)(2,1)S(1)}, bf16[256,256]{1,0:T(8,128)(2,1)S(1)}, u32[]{:S(2)}, u32[]{:S(2)}) collective-permute-start(bf16[256,256]{1,0:T(8,128)(2,1)S(1)} %get-tuple-element.232), channel_id=1, source_target_pairs={{60,0},{0,4},{4,8},{8,12},{12,16},{16,20},{20,24},{24,28},{28,32},... | collective-permute-start | bytes 393224 | tf_op jit(solution)/shard_map/while/body/eval_jaxpr/ppermute | solution.py:16
  120.5 9.9 %collective-permute-done = bf16[256,256]{1,0:T(8,128)(2,1)S(1)} collective-permute-done((bf16[256,256]{1,0:T(8,128)(2,1)S(1)}, bf16[256,256]{1,0:T(8,128)(2,1)S(1)}, u32[]{:S(2)}, u32[]{:S(2)}) %collective-permute-start) | collective-permute-done | bytes 131104 | tf_op jit(solution)/shard_map/while/body/eval_jaxpr/ppermute | solution.py:16
  133.9 5.0 collective-permute-done
  140.3 1.9 collective-permute-start
  142.2 5.0 collective-permute-done
  150.6 5.0 collective-permute-done
  159.0 5.0 collective-permute-done
  167.4 5.0 collective-permute-done
  175.8 5.8 %collective-permute-done = bf16[256,256]{1,0:T(8,128)(2,1)S(1)} collective-permute-done((bf16[256,256]{1,0:T(8,128)(2,1)S(1)}, bf16[256,256]{1,0:T(8,128)(2,1)S(1)}, u32[]{:S(2)}, u32[]{:S(2)}) %collective-permute-start) | collective-permute-done | bytes 131104 | tf_op jit(solution)/shard_map/while/body/eval_jaxpr/ppermute | solution.py:16
  185.0 6.1 %collective-permute-done = bf16[256,256]{1,0:T(8,128)(2,1)S(1)} collective-permute-done((bf16[256,256]{1,0:T(8,128)(2,1)S(1)}, bf16[256,256]{1,0:T(8,128)(2,1)S(1)}, u32[]{:S(2)}, u32[]{:S(2)}) %collective-permute-start) | collective-permute-done | bytes 131104 | tf_op jit(solution)/shard_map/while/body/eval_jaxpr/ppermute | solution.py:16
  192.5 1.9 collective-permute-start
  194.5 5.3 collective-permute-done
  203.2 5.0 collective-permute-done
  211.6 5.0 collective-permute-done
  219.9 5.0 collective-permute-done
  228.3 5.0 collective-permute-done
  236.7 5.0 collective-permute-done
  245.1 5.0 collective-permute-done
  257.4 36.2 %reduce-scatter.2.cloned.1.call-done = f32[256,256]{1,0:T(8,128)} async-done(((f32[256,1024]{1,0:T(8,128)}), f32[256,256]{1,0:T(8,128)}) %reduce-scatter.2.cloned.1.call-update) | async-done | bytes 262160 | tf_op jit(solution)/shard_map/reduce_scatter | solution.py:105
  295.8 105.2 %psum.7 = f32[512]{0:T(512)S(1)} all-reduce(f32[512]{0:T(512)S(1)} %bitcast.37), channel_id=1, replica_groups=mesh['row'=8,'col'=16,'layer'=4] {'row','col','layer'}, use_global_device_ids=true, to_apply=%region_6.7 | all-reduce | flops 512 | bytes 4096 | tf_op jit(solution)/shard_map/psum | solution.py:121
  403.7 3.1 collective-permute-start.1
  406.8 5.8 %collective-permute-start.2 = (f32[16,64,160]{2,1,0:T(8,128)S(1)}, f32[16,64,160]{2,1,0:T(8,128)S(1)}, u32[]{:S(2)}, u32[]{:S(2)}) collective-permute-start(f32[16,64,160]{2,1,0:T(8,128)S(1)} %get-tuple-element.176), channel_id=1, source_target_pairs={{64,0},{128,64},{192,128},{256,192},{320,256},{384,320},{448,384},... | collective-permute-start | bytes 1966088 | tf_op jit(solution)/shard_map/ppermute | solution.py:28
  412.6 20.6 %collective-permute-done.1 = f32[16,64,160]{2,1,0:T(8,128)S(1)} collective-permute-done((f32[16,64,160]{2,1,0:T(8,128)S(1)}, f32[16,64,160]{2,1,0:T(8,128)S(1)}, u32[]{:S(2)}, u32[]{:S(2)}) %collective-permute-start.1) | collective-permute-done | bytes 655392 | tf_op jit(solution)/shard_map/ppermute | solution.py:25
  433.3 19.8 %collective-permute-done.2 = f32[16,64,160]{2,1,0:T(8,128)S(1)} collective-permute-done((f32[16,64,160]{2,1,0:T(8,128)S(1)}, f32[16,64,160]{2,1,0:T(8,128)S(1)}, u32[]{:S(2)}, u32[]{:S(2)}) %collective-permute-start.2) | collective-permute-done | bytes 655392 | tf_op jit(solution)/shard_map/ppermute | solution.py:28
  454.7 3.3 copy.23
  458.0 2.9 collective-permute-start.4
  460.9 2.1 copy.22
  463.0 2.3 collective-permute-start.3
  465.3 23.6 %collective-permute-done.4 = f32[96,16,160]{0,2,1:T(8,128)} collective-permute-done((f32[96,16,160]{0,2,1:T(8,128)}, f32[96,16,160]{0,2,1:T(8,128)}, u32[]{:S(2)}, u32[]{:S(2)}) %collective-permute-start.4) | collective-permute-done | bytes 983072 | tf_op jit(solution)/shard_map/ppermute | solution.py:28
  489.0 2.6 copy.25
  491.6 3.4 collective-permute-done.3
  494.9 3.6 copy.24
  498.5 3.7 pad_maximum_fusion
  502.2 5.3 fusion.24
  507.5 3.8 copy.26
  511.3 4.4 collective-permute-start.5
  515.7 3.8 copy.27
  519.5 2.3 collective-permute-start.6
  521.8 3.2 collective-permute-done.5
  525.0 3.8 copy.28
  528.8 6.5 %collective-permute-done.6 = f32[96,96,16]{1,2,0:T(8,128)} collective-permute-done((f32[96,96,16]{1,2,0:T(8,128)}, f32[96,96,16]{1,2,0:T(8,128)}, u32[]{:S(2)}, u32[]{:S(2)}) %collective-permute-start.6) | collective-permute-done | bytes 589856 | tf_op jit(solution)/shard_map/ppermute | solution.py:28
  535.3 3.9 copy.29
  539.3 5.8 %maximum_add_fusion = f32[16,96,192]{2,1,0:T(8,128)S(1)} fusion(f32[96,96,16]{2,1,0:T(8,128)} %copy.29, f32[96,96,16]{2,1,0:T(8,128)} %copy.28, f32[96,16,160]{2,1,0:T(8,128)S(1)} %copy.25, f32[96,16,160]{2,1,0:T(8,128)} %copy.24, f32[16,64,160]{2,1,0:T(8,128)} %copy-done.4, f32[64,64,160]{2,1,0:T(8,128)} %copy-done, ...), kind=kLoop, calls=%fused_computation.21 | loop fusion | flops 3833856 | bytes 8257536 | tf_op jit(solution)/shard_map/add | solution.py:53
  546.1 4.0 fusion.3
  (101 shorter events, 62.2 us)
Async XLA Ops:
  7.2 1.2 copy-start.6
  12.9 8.6 %copy-start.7 = (bf16[256,256]{1,0:T(8,128)(2,1)S(1)}, bf16[256,256]{1,0:T(8,128)(2,1)}, u32[]{:S(2)}) copy-start(bf16[256,256]{1,0:T(8,128)(2,1)} %param.9) | copy-start | bytes 393220
  12.9 99.4 %all-to-all-start = ((bf16[8,512,1024]{2,1,0:T(8,128)(2,1)}), bf16[8,512,1024]{2,1,0:T(8,128)(2,1)}, u32[]{:S(2)}, u32[]{:S(2)}) async-start(bf16[8,512,1024]{2,1,0:T(8,128)(2,1)} %stack.3), calls=%async_computation | async-start | bytes 16777216 | tf_op jit(solution)/shard_map/all_to_all | solution.py:86
  20.5 273.2 %reduce-scatter.2.cloned.1.call-start = ((), (), s32[]{:S(2)}) async-start(), calls=%async_computation.2 | async-start | bytes 1310720 | tf_op jit(solution)/shard_map/reduce_scatter | solution.py:105
  113.7 16.8 %collective-permute-start = (bf16[256,256]{1,0:T(8,128)(2,1)S(1)}, bf16[256,256]{1,0:T(8,128)(2,1)S(1)}, u32[]{:S(2)}, u32[]{:S(2)}) collective-permute-start(bf16[256,256]{1,0:T(8,128)(2,1)S(1)} %get-tuple-element.232), channel_id=1, source_target_pairs={{60,0},{0,4},{4,8},{8,12},{12,16},{16,20},{20,24},{24,28},{28,32},... | collective-permute-start | bytes 393224 | tf_op jit(solution)/shard_map/while/body/eval_jaxpr/ppermute | solution.py:16
  131.9 6.9 %collective-permute-start = (bf16[256,256]{1,0:T(8,128)(2,1)S(1)}, bf16[256,256]{1,0:T(8,128)(2,1)S(1)}, u32[]{:S(2)}, u32[]{:S(2)}) collective-permute-start(bf16[256,256]{1,0:T(8,128)(2,1)S(1)} %get-tuple-element.232), channel_id=1, source_target_pairs={{60,0},{0,4},{4,8},{8,12},{12,16},{16,20},{20,24},{24,28},{28,32},... | collective-permute-start | bytes 393224 | tf_op jit(solution)/shard_map/while/body/eval_jaxpr/ppermute | solution.py:16
  140.3 6.9 %collective-permute-start = (bf16[256,256]{1,0:T(8,128)(2,1)S(1)}, bf16[256,256]{1,0:T(8,128)(2,1)S(1)}, u32[]{:S(2)}, u32[]{:S(2)}) collective-permute-start(bf16[256,256]{1,0:T(8,128)(2,1)S(1)} %get-tuple-element.232), channel_id=1, source_target_pairs={{60,0},{0,4},{4,8},{8,12},{12,16},{16,20},{20,24},{24,28},{28,32},... | collective-permute-start | bytes 393224 | tf_op jit(solution)/shard_map/while/body/eval_jaxpr/ppermute | solution.py:16
  148.7 6.9 %collective-permute-start = (bf16[256,256]{1,0:T(8,128)(2,1)S(1)}, bf16[256,256]{1,0:T(8,128)(2,1)S(1)}, u32[]{:S(2)}, u32[]{:S(2)}) collective-permute-start(bf16[256,256]{1,0:T(8,128)(2,1)S(1)} %get-tuple-element.232), channel_id=1, source_target_pairs={{60,0},{0,4},{4,8},{8,12},{12,16},{16,20},{20,24},{24,28},{28,32},... | collective-permute-start | bytes 393224 | tf_op jit(solution)/shard_map/while/body/eval_jaxpr/ppermute | solution.py:16
  157.1 6.9 %collective-permute-start = (bf16[256,256]{1,0:T(8,128)(2,1)S(1)}, bf16[256,256]{1,0:T(8,128)(2,1)S(1)}, u32[]{:S(2)}, u32[]{:S(2)}) collective-permute-start(bf16[256,256]{1,0:T(8,128)(2,1)S(1)} %get-tuple-element.232), channel_id=1, source_target_pairs={{60,0},{0,4},{4,8},{8,12},{12,16},{16,20},{20,24},{24,28},{28,32},... | collective-permute-start | bytes 393224 | tf_op jit(solution)/shard_map/while/body/eval_jaxpr/ppermute | solution.py:16
  165.4 6.9 %collective-permute-start = (bf16[256,256]{1,0:T(8,128)(2,1)S(1)}, bf16[256,256]{1,0:T(8,128)(2,1)S(1)}, u32[]{:S(2)}, u32[]{:S(2)}) collective-permute-start(bf16[256,256]{1,0:T(8,128)(2,1)S(1)} %get-tuple-element.232), channel_id=1, source_target_pairs={{60,0},{0,4},{4,8},{8,12},{12,16},{16,20},{20,24},{24,28},{28,32},... | collective-permute-start | bytes 393224 | tf_op jit(solution)/shard_map/while/body/eval_jaxpr/ppermute | solution.py:16
  173.8 7.7 %collective-permute-start = (bf16[256,256]{1,0:T(8,128)(2,1)S(1)}, bf16[256,256]{1,0:T(8,128)(2,1)S(1)}, u32[]{:S(2)}, u32[]{:S(2)}) collective-permute-start(bf16[256,256]{1,0:T(8,128)(2,1)S(1)} %get-tuple-element.232), channel_id=1, source_target_pairs={{60,0},{0,4},{4,8},{8,12},{12,16},{16,20},{20,24},{24,28},{28,32},... | collective-permute-start | bytes 393224 | tf_op jit(solution)/shard_map/while/body/eval_jaxpr/ppermute | solution.py:16
  183.0 8.1 %collective-permute-start = (bf16[256,256]{1,0:T(8,128)(2,1)S(1)}, bf16[256,256]{1,0:T(8,128)(2,1)S(1)}, u32[]{:S(2)}, u32[]{:S(2)}) collective-permute-start(bf16[256,256]{1,0:T(8,128)(2,1)S(1)} %get-tuple-element.232), channel_id=1, source_target_pairs={{60,0},{0,4},{4,8},{8,12},{12,16},{16,20},{20,24},{24,28},{28,32},... | collective-permute-start | bytes 393224 | tf_op jit(solution)/shard_map/while/body/eval_jaxpr/ppermute | solution.py:16
  192.5 7.2 %collective-permute-start = (bf16[256,256]{1,0:T(8,128)(2,1)S(1)}, bf16[256,256]{1,0:T(8,128)(2,1)S(1)}, u32[]{:S(2)}, u32[]{:S(2)}) collective-permute-start(bf16[256,256]{1,0:T(8,128)(2,1)S(1)} %get-tuple-element.232), channel_id=1, source_target_pairs={{60,0},{0,4},{4,8},{8,12},{12,16},{16,20},{20,24},{24,28},{28,32},... | collective-permute-start | bytes 393224 | tf_op jit(solution)/shard_map/while/body/eval_jaxpr/ppermute | solution.py:16
  201.2 6.9 %collective-permute-start = (bf16[256,256]{1,0:T(8,128)(2,1)S(1)}, bf16[256,256]{1,0:T(8,128)(2,1)S(1)}, u32[]{:S(2)}, u32[]{:S(2)}) collective-permute-start(bf16[256,256]{1,0:T(8,128)(2,1)S(1)} %get-tuple-element.232), channel_id=1, source_target_pairs={{60,0},{0,4},{4,8},{8,12},{12,16},{16,20},{20,24},{24,28},{28,32},... | collective-permute-start | bytes 393224 | tf_op jit(solution)/shard_map/while/body/eval_jaxpr/ppermute | solution.py:16
  209.6 6.9 %collective-permute-start = (bf16[256,256]{1,0:T(8,128)(2,1)S(1)}, bf16[256,256]{1,0:T(8,128)(2,1)S(1)}, u32[]{:S(2)}, u32[]{:S(2)}) collective-permute-start(bf16[256,256]{1,0:T(8,128)(2,1)S(1)} %get-tuple-element.232), channel_id=1, source_target_pairs={{60,0},{0,4},{4,8},{8,12},{12,16},{16,20},{20,24},{24,28},{28,32},... | collective-permute-start | bytes 393224 | tf_op jit(solution)/shard_map/while/body/eval_jaxpr/ppermute | solution.py:16
  218.0 6.9 %collective-permute-start = (bf16[256,256]{1,0:T(8,128)(2,1)S(1)}, bf16[256,256]{1,0:T(8,128)(2,1)S(1)}, u32[]{:S(2)}, u32[]{:S(2)}) collective-permute-start(bf16[256,256]{1,0:T(8,128)(2,1)S(1)} %get-tuple-element.232), channel_id=1, source_target_pairs={{60,0},{0,4},{4,8},{8,12},{12,16},{16,20},{20,24},{24,28},{28,32},... | collective-permute-start | bytes 393224 | tf_op jit(solution)/shard_map/while/body/eval_jaxpr/ppermute | solution.py:16
  226.4 6.9 %collective-permute-start = (bf16[256,256]{1,0:T(8,128)(2,1)S(1)}, bf16[256,256]{1,0:T(8,128)(2,1)S(1)}, u32[]{:S(2)}, u32[]{:S(2)}) collective-permute-start(bf16[256,256]{1,0:T(8,128)(2,1)S(1)} %get-tuple-element.232), channel_id=1, source_target_pairs={{60,0},{0,4},{4,8},{8,12},{12,16},{16,20},{20,24},{24,28},{28,32},... | collective-permute-start | bytes 393224 | tf_op jit(solution)/shard_map/while/body/eval_jaxpr/ppermute | solution.py:16
  234.8 6.9 %collective-permute-start = (bf16[256,256]{1,0:T(8,128)(2,1)S(1)}, bf16[256,256]{1,0:T(8,128)(2,1)S(1)}, u32[]{:S(2)}, u32[]{:S(2)}) collective-permute-start(bf16[256,256]{1,0:T(8,128)(2,1)S(1)} %get-tuple-element.232), channel_id=1, source_target_pairs={{60,0},{0,4},{4,8},{8,12},{12,16},{16,20},{20,24},{24,28},{28,32},... | collective-permute-start | bytes 393224 | tf_op jit(solution)/shard_map/while/body/eval_jaxpr/ppermute | solution.py:16
  243.1 6.9 %collective-permute-start = (bf16[256,256]{1,0:T(8,128)(2,1)S(1)}, bf16[256,256]{1,0:T(8,128)(2,1)S(1)}, u32[]{:S(2)}, u32[]{:S(2)}) collective-permute-start(bf16[256,256]{1,0:T(8,128)(2,1)S(1)} %get-tuple-element.232), channel_id=1, source_target_pairs={{60,0},{0,4},{4,8},{8,12},{12,16},{16,20},{20,24},{24,28},{28,32},... | collective-permute-start | bytes 393224 | tf_op jit(solution)/shard_map/while/body/eval_jaxpr/ppermute | solution.py:16
  251.5 2.0 copy-start.10
  251.5 3.3 copy-start.8
  251.5 3.7 copy-start.9
  403.6 49.5 %copy-start = (f32[64,64,160]{2,1,0:T(8,128)}, f32[64,64,160]{2,1,0:T(8,128)S(1)}, u32[]{:S(2)}) copy-start(f32[64,64,160]{2,1,0:T(8,128)S(1)} %broadcast_multiply_fusion) | copy-start | bytes 7864324
  403.7 29.6 %collective-permute-start.1 = (f32[16,64,160]{2,1,0:T(8,128)S(1)}, f32[16,64,160]{2,1,0:T(8,128)S(1)}, u32[]{:S(2)}, u32[]{:S(2)}) collective-permute-start(f32[16,64,160]{2,1,0:T(8,128)S(1)} %get-tuple-element.175), channel_id=1, source_target_pairs={{0,64},{64,128},{128,192},{192,256},{256,320},{320,384},{384,448},... | collective-permute-start | bytes 1966088 | tf_op jit(solution)/shard_map/ppermute | solution.py:25
  406.8 46.3 %collective-permute-start.2 = (f32[16,64,160]{2,1,0:T(8,128)S(1)}, f32[16,64,160]{2,1,0:T(8,128)S(1)}, u32[]{:S(2)}, u32[]{:S(2)}) collective-permute-start(f32[16,64,160]{2,1,0:T(8,128)S(1)} %get-tuple-element.176), channel_id=1, source_target_pairs={{64,0},{128,64},{192,128},{256,192},{320,256},{384,320},{448,384},... | collective-permute-start | bytes 1966088 | tf_op jit(solution)/shard_map/ppermute | solution.py:28
  453.1 1.6 copy-start.4
  458.0 31.0 %collective-permute-start.4 = (f32[96,16,160]{0,2,1:T(8,128)}, f32[96,16,160]{0,2,1:T(8,128)}, u32[]{:S(2)}, u32[]{:S(2)}) collective-permute-start(f32[96,16,160]{0,2,1:T(8,128)} %copy.23), channel_id=1, source_target_pairs={{4,0},{8,4},{12,8},{16,12},{20,16},{24,20},{28,24},{32,28},{36,32}... | collective-permute-start | bytes 2949128 | tf_op jit(solution)/shard_map/ppermute | solution.py:28
  463.0 31.9 %collective-permute-start.3 = (f32[96,16,160]{0,2,1:T(8,128)}, f32[96,16,160]{0,2,1:T(8,128)}, u32[]{:S(2)}, u32[]{:S(2)}) collective-permute-start(f32[96,16,160]{0,2,1:T(8,128)} %copy.22), channel_id=1, source_target_pairs={{0,4},{4,8},{8,12},{12,16},{16,20},{20,24},{24,28},{28,32},{32,36}... | collective-permute-start | bytes 2949128 | tf_op jit(solution)/shard_map/ppermute | solution.py:25
  511.3 13.7 %collective-permute-start.5 = (f32[96,96,16]{1,2,0:T(8,128)}, f32[96,96,16]{1,2,0:T(8,128)}, u32[]{:S(2)}, u32[]{:S(2)}) collective-permute-start(f32[96,96,16]{1,2,0:T(8,128)} %copy.26), channel_id=1, source_target_pairs={{0,1},{1,2},{2,3},{3,0},{4,5},{5,6},{6,7},{7,4},{8,9},{9,10},{10,1... | collective-permute-start | bytes 1769480 | tf_op jit(solution)/shard_map/ppermute | solution.py:25
  519.5 15.8 %collective-permute-start.6 = (f32[96,96,16]{1,2,0:T(8,128)}, f32[96,96,16]{1,2,0:T(8,128)}, u32[]{:S(2)}, u32[]{:S(2)}) collective-permute-start(f32[96,96,16]{1,2,0:T(8,128)} %copy.27), channel_id=1, source_target_pairs={{1,0},{2,1},{3,2},{0,3},{5,4},{6,5},{7,6},{4,7},{9,8},{10,9},{11,1... | collective-permute-start | bytes 1769480 | tf_op jit(solution)/shard_map/ppermute | solution.py:28
  535.3 9.8 %slice-start = ((s8[4718592]{0:T(1024)(128)(4,1)}), s8[524288]{0:T(1024)(128)(4,1)S(1)}, s32[]{:S(2)}) async-start(s8[4718592]{0:T(1024)(128)(4,1)} %bitcast.32), calls=%async_computation.3 | async-start | bytes 1048576
  539.3 5.9 %copy-start.1 = (f32[64,64,160]{2,1,0:T(8,128)S(1)}, f32[64,64,160]{2,1,0:T(8,128)}, u32[]{:S(2)}) copy-start(f32[64,64,160]{2,1,0:T(8,128)} %copy-done) | copy-start | bytes 7864324
  539.3 5.9 %slice-start.1 = ((s8[4718592]{0:T(1024)(128)(4,1)}), s8[4194304]{0:T(1024)(128)(4,1)S(1)}, s32[]{:S(2)}) async-start(s8[4718592]{0:T(1024)(128)(4,1)} %bitcast.32), calls=%async_computation.4 | async-start | bytes 8388608
  539.3 6.2 %copy-start.2 = (f32[96,96,16]{2,1,0:T(8,128)S(1)}, f32[96,96,16]{2,1,0:T(8,128)}, u32[]{:S(2)}) copy-start(f32[96,96,16]{2,1,0:T(8,128)} %copy.29) | copy-start | bytes 1769476
  539.3 6.6 %copy-start.3 = (f32[96,16,160]{2,1,0:T(8,128)S(1)}, f32[96,16,160]{2,1,0:T(8,128)}, u32[]{:S(2)}) copy-start(f32[96,16,160]{2,1,0:T(8,128)} %copy.24) | copy-start | bytes 2949124
  539.3 6.9 %copy-start.5 = (f32[16,64,160]{2,1,0:T(8,128)S(1)}, f32[16,64,160]{2,1,0:T(8,128)}, u32[]{:S(2)}) copy-start(f32[16,64,160]{2,1,0:T(8,128)} %copy-done.4) | copy-start | bytes 1966084
Sparse Core Ops, SparseCore 0:
  253.0 40.6 reduce-scatter.1
